TPU v7x, 32 devices: a whole 2x2x4 slice. The times are simulated.
32 devices in a mesh: dates: 8 (over z, y), tiles: 4 (over x, core).
Axes of the slice: x: 2, y: 2, z: 4, core: 2. Of those that a mesh axis runs over, the one named last changes fastest.
Arguments:
- observed: float32 [256, 32, 1024], P('dates', None, 'tiles'), may hold values from -12 to 12
- cloud_mask: int32 [256, 32, 1024], P('dates', None, 'tiles'), may hold values from 0 to 3
- diffuse_rows: float32 [32, 1024], P(None, 'tiles'), may hold values from 0.02 to 0.24
- diffuse_cols: float32 [32, 1024], P(None, 'tiles'), may hold values from 0.02 to 0.24
Outputs:
- filled: float32 [256, 32, 1024], P('dates', None, 'tiles')
All inputs are finite; a program needn't handle non-finite values.
Results may differ from a plain program's by a relative error of at most 0.0003.
Values sent between devices are 32-bit elements; how exact they have to be, the bound alone decides.
A program may use at most 64 MiB of HBM per device.

v0:
```python
import jax
import jax.numpy as jnp
from jax import lax
from jax.sharding import PartitionSpec as P

ITERS = 10
STEPS = 4


smooth_weight = 4.0


def padded_2(cells, sides, width):
    for axis, dim in sides:
        count = lax.axis_size(axis)
        ends = count - 1
        head = lax.slice_in_dim(cells, 0, width, axis=dim)
        tail = lax.slice_in_dim(cells, cells.shape[dim] - width, cells.shape[dim], axis=dim)
        cells = jnp.concatenate(
            [
                lax.ppermute(tail, axis, [(i, (i + 1) % count) for i in range(ends)]),
                cells,
                lax.ppermute(head, axis, [((i + 1) % count, i) for i in range(ends)]),
            ],
            axis=dim,
        )
    return cells


def time_operator(values, weights):
    second = values[:-2] - 2.0 * values[1:-1] + values[2:]
    padded = jnp.pad(second, ((2, 2), (0, 0), (0, 0)))
    back = padded[:-2] - 2.0 * padded[1:-1] + padded[2:]
    return weights * values + smooth_weight * back


def squares(residual):
    return lax.psum(jnp.sum(residual * residual), ("dates", "tiles"))


def solve_series(rhs, weights):
    smoothed = jnp.zeros_like(rhs)

    def advance(step, state):
        smoothed, residual, direction, norm_now = state
        image = time_operator(direction, weights)
        curve = lax.psum(jnp.sum(direction * image), ("dates", "tiles"))
        alpha = norm_now / curve
        smoothed = smoothed + alpha * direction
        residual = residual - alpha * image
        fresh = squares(residual)
        direction = residual + fresh / norm_now * direction
        return (smoothed, residual, direction, fresh)

    state = (smoothed, rhs, rhs, squares(rhs))
    state = lax.fori_loop(0, ITERS, advance, state)
    return state[0]


def body(observed, cloud_mask, diffuse_rows, diffuse_cols):
    weights = cloud_mask.astype(jnp.float32) / 3.0 + 0.05
    rhs = weights * observed
    rhs_rows, weight_rows = (
        lax.all_to_all(rhs, "dates", split_axis=1, concat_axis=0, tiled=True),
        lax.all_to_all(weights, "dates", split_axis=1, concat_axis=0, tiled=True),
    )
    smoothed = solve_series(rhs_rows, weight_rows)
    filled = lax.all_to_all(smoothed, "dates", split_axis=0, concat_axis=1, tiled=True)
    for step in range(STEPS):
        widened = padded_2(filled, (("tiles", 2),), 1)
        padded = jnp.pad(widened, ((0, 0), (1, 1), (0, 0)))
        centre = padded[:, 1:-1, 1:-1]
        along_rows = padded[:, 2:, 1:-1] + padded[:, :-2, 1:-1] - 2.0 * centre
        along_cols = padded[:, 1:-1, 2:] + padded[:, 1:-1, :-2] - 2.0 * centre
        filled = filled + diffuse_rows * along_rows + diffuse_cols * along_cols
    return filled


def solution(mesh):
    in_specs = (
        P("dates", None, "tiles"),
        P("dates", None, "tiles"),
        P(None, "tiles"),
        P(None, "tiles"),
    )
    out_specs = P("dates", None, "tiles")
    return jax.shard_map(body, mesh=mesh, in_specs=in_specs, out_specs=out_specs, check_vma=False)
```

profile of v0, /device:TPU:0, one launch (start us, length us, event | category | flops | bytes accessed | tf_op | source)
XLA Modules:
  0.0 1082.5 jit_solution(11180577021034416808)
XLA Ops:
  0.0 3.9 fusion.30
  3.9 32.8 %all_to_all.54 = f32[32,32,256]{2,0,1:T(8,128)S(1)} all-to-all(f32[32,32,256]{2,0,1:T(8,128)S(1)} %get-tuple-element.131), channel_id=1, replica_groups=mesh['dates'=8,'tiles'=4] {'dates'}, dimensions={1} | all-to-all | bytes 2097152 | tf_op jit(solution)/shard_map/all_to_all | solution.py:64
  36.7 3.6 all-to-all-start.1
  41.9 24.0 %all-to-all-done.1 = f32[32,32,256]{2,0,1:T(8,128)S(1)} async-done(((f32[32,32,256]{2,0,1:T(8,128)}), f32[32,32,256]{2,0,1:T(8,128)S(1)}, u32[]{:S(2)}, u32[]{:S(2)}) %all-to-all-start.1) | async-done | bytes 1048608 | tf_op jit(solution)/shard_map/all_to_all | solution.py:65
  67.5 37.9 %psum.27 = f32[]{:T(128)} all-reduce(f32[]{:T(128)} %multiply_reduce_fusion.2), channel_id=1, replica_groups=mesh['dates'=8,'tiles'=4] {'dates','tiles'}, use_global_device_ids=true, to_apply=%region_1.0 | all-reduce | flops 1 | bytes 8 | tf_op jit(solution)/shard_map/psum | solution.py:38
  105.6 894.8 %while.19 = (s32[]{:T(128)}, f32[256,4,256]{2,1,0:T(4,128)}, f32[256,4,256]{2,1,0:T(4,128)S(1)}, f32[256,4,256]{2,1,0:T(4,128)S(1)}, f32[]{:T(128)}, /*index=5*/f32[256,4,256]{2,1,0:T(4,128)}, s32[]{:T(128)}, s32[]{:T(128)}) while((s32[]{:T(128)}, f32[256,4,256]{2,1,0:T(4,128)}, f32[256,4,256]{2,1,0:T(4,128)S(1)}, ...), condition=%wide.region_7.8_spmd.clone, body=%wide.region_2.7_spmd.clone.sunk | while | flops 5236741 | bytes 20930752 | solution.py:56
  108.8 42.0 %psum.32 = f32[]{:T(128)} all-reduce(f32[]{:T(128)} %get-tuple-element.176), channel_id=1, replica_groups=mesh['dates'=8,'tiles'=4] {'dates','tiles'}, use_global_device_ids=true, to_apply=%region_4.4 | all-reduce | flops 1 | bytes 8 | tf_op jit(solution)/shard_map/while/body/eval_jaxpr/psum | solution.py:47
  152.7 39.5 %psum.33 = f32[]{:T(128)} all-reduce(f32[]{:T(128)} %get-tuple-element.178), channel_id=1, replica_groups=mesh['dates'=8,'tiles'=4] {'dates','tiles'}, use_global_device_ids=true, to_apply=%region_6.6 | all-reduce | flops 1 | bytes 8 | tf_op jit(solution)/shard_map/while/body/eval_jaxpr/psum | solution.py:38
  197.8 41.3 %psum.32 = f32[]{:T(128)} all-reduce(f32[]{:T(128)} %get-tuple-element.176), channel_id=1, replica_groups=mesh['dates'=8,'tiles'=4] {'dates','tiles'}, use_global_device_ids=true, to_apply=%region_4.4 | all-reduce | flops 1 | bytes 8 | tf_op jit(solution)/shard_map/while/body/eval_jaxpr/psum | solution.py:47
  241.0 39.5 %psum.33 = f32[]{:T(128)} all-reduce(f32[]{:T(128)} %get-tuple-element.178), channel_id=1, replica_groups=mesh['dates'=8,'tiles'=4] {'dates','tiles'}, use_global_device_ids=true, to_apply=%region_6.6 | all-reduce | flops 1 | bytes 8 | tf_op jit(solution)/shard_map/while/body/eval_jaxpr/psum | solution.py:38
  281.2 2.9 multiply_add_fusion.4
  287.3 41.3 %psum.32 = f32[]{:T(128)} all-reduce(f32[]{:T(128)} %get-tuple-element.176), channel_id=1, replica_groups=mesh['dates'=8,'tiles'=4] {'dates','tiles'}, use_global_device_ids=true, to_apply=%region_4.4 | all-reduce | flops 1 | bytes 8 | tf_op jit(solution)/shard_map/while/body/eval_jaxpr/psum | solution.py:47
  330.5 39.5 %psum.33 = f32[]{:T(128)} all-reduce(f32[]{:T(128)} %get-tuple-element.178), channel_id=1, replica_groups=mesh['dates'=8,'tiles'=4] {'dates','tiles'}, use_global_device_ids=true, to_apply=%region_6.6 | all-reduce | flops 1 | bytes 8 | tf_op jit(solution)/shard_map/while/body/eval_jaxpr/psum | solution.py:38
  376.9 41.3 %psum.32 = f32[]{:T(128)} all-reduce(f32[]{:T(128)} %get-tuple-element.176), channel_id=1, replica_groups=mesh['dates'=8,'tiles'=4] {'dates','tiles'}, use_global_device_ids=true, to_apply=%region_4.4 | all-reduce | flops 1 | bytes 8 | tf_op jit(solution)/shard_map/while/body/eval_jaxpr/psum | solution.py:47
  420.1 39.5 %psum.33 = f32[]{:T(128)} all-reduce(f32[]{:T(128)} %get-tuple-element.178), channel_id=1, replica_groups=mesh['dates'=8,'tiles'=4] {'dates','tiles'}, use_global_device_ids=true, to_apply=%region_6.6 | all-reduce | flops 1 | bytes 8 | tf_op jit(solution)/shard_map/while/body/eval_jaxpr/psum | solution.py:38
  466.4 41.3 %psum.32 = f32[]{:T(128)} all-reduce(f32[]{:T(128)} %get-tuple-element.176), channel_id=1, replica_groups=mesh['dates'=8,'tiles'=4] {'dates','tiles'}, use_global_device_ids=true, to_apply=%region_4.4 | all-reduce | flops 1 | bytes 8 | tf_op jit(solution)/shard_map/while/body/eval_jaxpr/psum | solution.py:47
  509.6 39.5 %psum.33 = f32[]{:T(128)} all-reduce(f32[]{:T(128)} %get-tuple-element.178), channel_id=1, replica_groups=mesh['dates'=8,'tiles'=4] {'dates','tiles'}, use_global_device_ids=true, to_apply=%region_6.6 | all-reduce | flops 1 | bytes 8 | tf_op jit(solution)/shard_map/while/body/eval_jaxpr/psum | solution.py:38
  555.9 41.3 %psum.32 = f32[]{:T(128)} all-reduce(f32[]{:T(128)} %get-tuple-element.176), channel_id=1, replica_groups=mesh['dates'=8,'tiles'=4] {'dates','tiles'}, use_global_device_ids=true, to_apply=%region_4.4 | all-reduce | flops 1 | bytes 8 | tf_op jit(solution)/shard_map/while/body/eval_jaxpr/psum | solution.py:47
  599.1 39.5 %psum.33 = f32[]{:T(128)} all-reduce(f32[]{:T(128)} %get-tuple-element.178), channel_id=1, replica_groups=mesh['dates'=8,'tiles'=4] {'dates','tiles'}, use_global_device_ids=true, to_apply=%region_6.6 | all-reduce | flops 1 | bytes 8 | tf_op jit(solution)/shard_map/while/body/eval_jaxpr/psum | solution.py:38
  645.5 41.3 %psum.32 = f32[]{:T(128)} all-reduce(f32[]{:T(128)} %get-tuple-element.176), channel_id=1, replica_groups=mesh['dates'=8,'tiles'=4] {'dates','tiles'}, use_global_device_ids=true, to_apply=%region_4.4 | all-reduce | flops 1 | bytes 8 | tf_op jit(solution)/shard_map/while/body/eval_jaxpr/psum | solution.py:47
  688.7 39.5 %psum.33 = f32[]{:T(128)} all-reduce(f32[]{:T(128)} %get-tuple-element.178), channel_id=1, replica_groups=mesh['dates'=8,'tiles'=4] {'dates','tiles'}, use_global_device_ids=true, to_apply=%region_6.6 | all-reduce | flops 1 | bytes 8 | tf_op jit(solution)/shard_map/while/body/eval_jaxpr/psum | solution.py:38
  735.0 41.3 %psum.32 = f32[]{:T(128)} all-reduce(f32[]{:T(128)} %get-tuple-element.176), channel_id=1, replica_groups=mesh['dates'=8,'tiles'=4] {'dates','tiles'}, use_global_device_ids=true, to_apply=%region_4.4 | all-reduce | flops 1 | bytes 8 | tf_op jit(solution)/shard_map/while/body/eval_jaxpr/psum | solution.py:47
  778.2 39.5 %psum.33 = f32[]{:T(128)} all-reduce(f32[]{:T(128)} %get-tuple-element.178), channel_id=1, replica_groups=mesh['dates'=8,'tiles'=4] {'dates','tiles'}, use_global_device_ids=true, to_apply=%region_6.6 | all-reduce | flops 1 | bytes 8 | tf_op jit(solution)/shard_map/while/body/eval_jaxpr/psum | solution.py:38
  824.5 41.3 %psum.32 = f32[]{:T(128)} all-reduce(f32[]{:T(128)} %get-tuple-element.176), channel_id=1, replica_groups=mesh['dates'=8,'tiles'=4] {'dates','tiles'}, use_global_device_ids=true, to_apply=%region_4.4 | all-reduce | flops 1 | bytes 8 | tf_op jit(solution)/shard_map/while/body/eval_jaxpr/psum | solution.py:47
  867.7 39.5 %psum.33 = f32[]{:T(128)} all-reduce(f32[]{:T(128)} %get-tuple-element.178), channel_id=1, replica_groups=mesh['dates'=8,'tiles'=4] {'dates','tiles'}, use_global_device_ids=true, to_apply=%region_6.6 | all-reduce | flops 1 | bytes 8 | tf_op jit(solution)/shard_map/while/body/eval_jaxpr/psum | solution.py:38
  914.1 41.3 %psum.32 = f32[]{:T(128)} all-reduce(f32[]{:T(128)} %get-tuple-element.176), channel_id=1, replica_groups=mesh['dates'=8,'tiles'=4] {'dates','tiles'}, use_global_device_ids=true, to_apply=%region_4.4 | all-reduce | flops 1 | bytes 8 | tf_op jit(solution)/shard_map/while/body/eval_jaxpr/psum | solution.py:47
  957.3 39.5 %psum.33 = f32[]{:T(128)} all-reduce(f32[]{:T(128)} %get-tuple-element.178), channel_id=1, replica_groups=mesh['dates'=8,'tiles'=4] {'dates','tiles'}, use_global_device_ids=true, to_apply=%region_6.6 | all-reduce | flops 1 | bytes 8 | tf_op jit(solution)/shard_map/while/body/eval_jaxpr/psum | solution.py:38
  1000.4 29.7 %all_to_all.55 = f32[256,4,256]{2,1,0:T(4,128)S(1)} all-to-all(f32[256,4,256]{2,1,0:T(4,128)} %get-tuple-element.82), channel_id=1, replica_groups=mesh['dates'=8,'tiles'=4] {'dates'}, dimensions={0} | all-to-all | bytes 2097152 | tf_op jit(solution)/shard_map/all_to_all | solution.py:68
  1032.3 3.1 collective-permute-start
  1040.5 8.2 collective-permute-start.2
  1053.6 9.6 collective-permute-start.4
  1068.3 9.6 collective-permute-start.6
  (94 shorter events, 88.3 us)
Async XLA Ops:
  36.7 29.2 %all-to-all-start.1 = ((f32[32,32,256]{2,0,1:T(8,128)}), f32[32,32,256]{2,0,1:T(8,128)S(1)}, u32[]{:S(2)}, u32[]{:S(2)}) async-start(f32[32,32,256]{2,0,1:T(8,128)} %get-tuple-element.130), calls=%async_computation.1 | async-start | bytes 2097152 | tf_op jit(solution)/shard_map/all_to_all | solution.py:65
  106.2 1.2 copy-start
  195.2 1.2 copy-start
  284.7 1.2 copy-start
  374.3 1.2 copy-start
  463.8 1.2 copy-start
  553.3 1.2 copy-start
  642.9 1.2 copy-start
  732.4 1.2 copy-start
  822.0 1.2 copy-start
  911.5 1.2 copy-start
  1031.0 4.4 collective-permute-start.1
  1032.3 5.4 copy-start.1
  1032.3 5.4 copy-start.2
  1032.3 4.6 collective-permute-start
  1039.2 9.5 collective-permute-start.3
  1040.5 9.5 collective-permute-start.2
  1052.3 10.9 %collective-permute-start.5 = (f32[32,32,1]{2,1,0:T(8,128)S(1)}, f32[32,32,1]{2,1,0:T(8,128)S(1)}, u32[]{:S(2)}, u32[]{:S(2)}) collective-permute-start(f32[32,32,1]{2,1,0:T(8,128)S(1)} %get-tuple-element.124), channel_id=1, source_target_pairs={{1,0},{2,1},{3,2},{5,4},{6,5},{7,6},{9,8},{10,9},{11,10},{13,12},{... | collective-permute-start | bytes 12296 | tf_op jit(solution)/shard_map/ppermute | solution.py:23
  1053.6 11.1 %collective-permute-start.4 = (f32[32,32,1]{2,1,0:T(8,128)S(1)}, f32[32,32,1]{2,1,0:T(8,128)S(1)}, u32[]{:S(2)}, u32[]{:S(2)}) collective-permute-start(f32[32,32,1]{2,1,0:T(8,128)S(1)} %get-tuple-element.125), channel_id=1, source_target_pairs={{0,1},{1,2},{2,3},{4,5},{5,6},{6,7},{8,9},{9,10},{10,11},{12,13},{... | collective-permute-start | bytes 12296 | tf_op jit(solution)/shard_map/ppermute | solution.py:21
  1067.0 10.9 %collective-permute-start.7 = (f32[32,32,1]{2,1,0:T(8,128)S(1)}, f32[32,32,1]{2,1,0:T(8,128)S(1)}, u32[]{:S(2)}, u32[]{:S(2)}) collective-permute-start(f32[32,32,1]{2,1,0:T(8,128)S(1)} %get-tuple-element.122), channel_id=1, source_target_pairs={{1,0},{2,1},{3,2},{5,4},{6,5},{7,6},{9,8},{10,9},{11,10},{13,12},{... | collective-permute-start | bytes 12296 | tf_op jit(solution)/shard_map/ppermute | solution.py:23
  1068.3 11.1 %collective-permute-start.6 = (f32[32,32,1]{2,1,0:T(8,128)S(1)}, f32[32,32,1]{2,1,0:T(8,128)S(1)}, u32[]{:S(2)}, u32[]{:S(2)}) collective-permute-start(f32[32,32,1]{2,1,0:T(8,128)S(1)} %get-tuple-element.123), channel_id=1, source_target_pairs={{0,1},{1,2},{2,3},{4,5},{5,6},{6,7},{8,9},{9,10},{10,11},{12,13},{... | collective-permute-start | bytes 12296 | tf_op jit(solution)/shard_map/ppermute | solution.py:21
where the time goes:
time: 1090 us; the launch traced here: 1080 us
  blocking collectives  909 us (83%)
  other arithmetic  70.3 us (6%)
  starting transfers between devices  39.3 us (4%)
  waiting for transfers between devices  29.7 us (3%)
  loops' own time  19.9 us (2%)
  local copies, waits for them, and re-layouts  13.8 us (1%)
    psum x11, blocking collectives, squares(): return lax.psum(jnp.sum(residual * residual), ('dates', 'tiles'))  433 us
    psum x10, blocking collectives, advance(): curve = lax.psum(jnp.sum(direction * image), ('dates', 'tiles'))  414 us
    all_to_all x1, blocking collectives, body(): lax.all_to_all(rhs, 'dates', split_axis=1, concat_axis=0, tiled=True)  32.8 us
    ppermute x4, starting transfers between devices, padded_2(): lax.ppermute(tail, axis, [(i, (i + 1) % count) for i in range(ends)])  30.6 us
    all_to_all x1, blocking collectives, body(): lax.all_to_all(smoothed, 'dates', split_axis=0, concat_axis=1, tiled=True)  29.7 us
    add x10, other arithmetic, advance(): direction = residual + fresh / norm_now * direction  28.2 us
    all_to_all x1, waiting for transfers between devices, body(): lax.all_to_all(weights, 'dates', split_axis=1, concat_axis=0, tiled=True)  24 us
  transfers between devices with their start and end apart: 9, of which 5 were waited for; matrix products, arithmetic and copies ran while one was open for 0% of the time, Pallas kernels for 0%

commit v1 on v0

v1 whole, which is shorter than its diff:
```python
import functools

import jax
import jax.numpy as jnp
from jax import lax
from jax.experimental import pallas as pl
from jax.experimental.pallas import tpu as pltpu
from jax.sharding import PartitionSpec as P

ITERS = 10
STEPS = 4
LANES = 128
SUB = 8
ROWS_AT_ONCE = 32

smooth_weight = 4.0
LOW, HIGH = 0.05, 65.05
MID, HALF = (LOW + HIGH) / 2, (HIGH - LOW) / 2
PIVOT_MIN = 0.02
MESH = pl.DeviceIdType.MESH


def kernel(nd, nt, chunks, obs_ref, mask_ref, dr_ref, dc_ref, out_ref, flag_ref,
           basis, weights, pack_out, pack_in, coef_in, coefs, acc_ref, sum_a, sum_b, nu_ref, c_ref, halo_ref,
           halo_send, halo_recv, pack_send, pack_recv, coef_send, coef_recv, a_send, a_recv, b_send, b_recv):
    D, R, C = obs_ref.shape
    RC = R // chunks
    me_d, me_t = lax.axis_index("dates"), lax.axis_index("tiles")
    has_l, has_r = me_d > 0, me_d < nd - 1
    has_w, has_e = me_t > 0, me_t < nt - 1
    mask_l = jnp.where(has_l, 1.0, 0.0).astype(jnp.float32)
    mask_r = jnp.where(has_r, 1.0, 0.0).astype(jnp.float32)

    barrier = pltpu.get_barrier_semaphore()
    for o in range(1, nt):
        pl.semaphore_signal(barrier, inc=1, device_id={"tiles": lax.rem(me_t + o, nt)}, device_id_type=MESH)
    for o in range(1, nd):
        pl.semaphore_signal(barrier, inc=1, device_id={"dates": lax.rem(me_d + o, nd)}, device_id_type=MESH)

    def start_plane(t, _):
        w = mask_ref[t].astype(jnp.float32) / 3.0 + 0.05
        weights[t] = w
        basis[0, t + 2] = w * obs_ref[t]
        return 0

    lax.fori_loop(0, D, start_plane, 0)

    def clear(ref, ks, at):
        def one(k, _):
            ref[(k,) + at] = jnp.zeros_like(ref[(k,) + at])
            return 0
        lax.fori_loop(0, ks, one, 0)

    @pl.when(jnp.logical_not(has_l))
    def _():
        clear(basis, ITERS, (pl.ds(0, 2),))

    @pl.when(jnp.logical_not(has_r))
    def _():
        clear(basis, ITERS, (pl.ds(D + 2, 2),))

    @pl.when(jnp.logical_not(has_e))
    def _():
        clear(pack_in, ITERS, (0,))
        coef_in[0] = jnp.zeros_like(coef_in[0])

    @pl.when(jnp.logical_not(has_w))
    def _():
        clear(pack_in, ITERS, (1,))
        coef_in[1] = jnp.zeros_like(coef_in[1])

    pl.semaphore_wait(barrier, nt - 1 + nd - 1)

    def halo_copy(k, c, side):
        rows = pl.ds(c * RC, RC)
        if side == 0:
            src, dst, to = basis.at[k, pl.ds(D, 2), rows], basis.at[k, pl.ds(0, 2), rows], me_d + 1
        else:
            src, dst, to = basis.at[k, pl.ds(2, 2), rows], basis.at[k, pl.ds(D + 2, 2), rows], me_d - 1
        return pltpu.make_async_remote_copy(
            src_ref=src, dst_ref=dst, send_sem=halo_send.at[k, c, side], recv_sem=halo_recv.at[k, c, side],
            device_id={"dates": to}, device_id_type=MESH)

    def pack_copy(k, side):
        return pltpu.make_async_remote_copy(
            src_ref=pack_out.at[k, side], dst_ref=pack_in.at[k, side], send_sem=pack_send.at[k, side],
            recv_sem=pack_recv.at[k, side], device_id={"tiles": me_t - 1 if side == 0 else me_t + 1}, device_id_type=MESH)

    def coef_copy(which, side):
        ref = (dr_ref, dc_ref)[which]
        cols = pl.ds(0 if side == 0 else C - LANES, LANES)
        return pltpu.make_async_remote_copy(
            src_ref=ref.at[:, cols], dst_ref=coef_in.at[side, which], send_sem=coef_send.at[side, which],
            recv_sem=coef_recv.at[side, which], device_id={"tiles": me_t - 1 if side == 0 else me_t + 1}, device_id_type=MESH)

    def send_halo(k, c):
        @pl.when(has_r)
        def _():
            halo_copy(k, c, 0).start()

        @pl.when(has_l)
        def _():
            halo_copy(k, c, 1).start()

    def wait_halo(k, c):
        @pl.when(has_l)
        def _():
            halo_copy(k, c, 0).wait_recv()

        @pl.when(has_r)
        def _():
            halo_copy(k, c, 1).wait_recv()

    for c in range(chunks):
        send_halo(0, c)

    @pl.when(has_w)
    def _():
        for which in range(2):
            coef_copy(which, 0).start()

    @pl.when(has_e)
    def _():
        for which in range(2):
            coef_copy(which, 1).start()

    def second(v, j):
        u = v[j] - 2.0 * v[j + 1] + v[j + 2]
        if j < 0:
            u = u * mask_l
        if j >= D - 2:
            u = u * mask_r
        return u

    def next_plane(k, t, rows, v, u, first):
        back = u[t - 2] - 2.0 * u[t - 1] + u[t]
        image = weights[t, rows] * v[t] + smooth_weight * back
        scale = 1.0 if first else 2.0
        new = (scale / HALF) * image - (scale * MID / HALF) * v[t]
        if not first:
            new = new - basis[k - 1, t + 2, rows]
        return new

    edges = sorted({0, 1, D - 2, D - 1})

    def edge_step(k, c, first):
        def part(r, _):
            rows = pl.ds(pl.multiple_of(c * RC + r * SUB, SUB), SUB)
            v, u = {}, {}
            for t in edges:
                for j in range(t - 2, t + 3):
                    if j not in v:
                        v[j] = basis[k, j + 2, rows]
                for j in range(t - 2, t + 1):
                    if j not in u:
                        u[j] = second(v, j)
                basis[k + 1, t + 2, rows] = next_plane(k, t, rows, v, u, first)
            return 0
        if RC == SUB:
            part(0, 0)
        else:
            lax.fori_loop(0, RC // SUB, part, 0)

    def inner_step(k, first, last):
        def part(r, carry):
            own, cross = carry
            rows = pl.ds(pl.multiple_of(r * SUB, SUB), SUB)
            v, u = {}, {}
            for t in range(D):
                stored = t in edges and not last
                for j in range(t - 2, t + 3):
                    if j not in v and not (stored and j != t):
                        v[j] = basis[k, j + 2, rows]
                if stored:
                    new = basis[k + 1, t + 2, rows]
                else:
                    for j in range(t - 2, t + 1):
                        if j not in u:
                            u[j] = second(v, j)
                    new = next_plane(k, t, rows, v, u, first)
                    if not last:
                        basis[k + 1, t + 2, rows] = new
                own = own + v[t] * v[t]
                cross = cross + v[t] * new
            return own, cross
        zero = jnp.zeros((SUB, C), jnp.float32)
        own, cross = lax.fori_loop(0, R // SUB, part, (zero, zero))
        for which, acc in ((0, own), (1, cross)):
            acc_ref[k, which] = functools.reduce(lambda a, b: a + b, [acc[:, i:i + LANES] for i in range(0, C, LANES)])

    lane = lax.broadcasted_iota(jnp.int32, (ROWS_AT_ONCE, LANES), 1)
    group = lane // STEPS
    groups = LANES // STEPS

    def pack_step(k):
        def part(r, _):
            rows = pl.ds(pl.multiple_of(r * ROWS_AT_ONCE, ROWS_AT_ONCE), ROWS_AT_ONCE)
            west = east = jnp.zeros((ROWS_AT_ONCE, LANES), jnp.float32)
            for d in range(D):
                both = jnp.where(lane < LANES // 2, basis[k, d + 2, rows, pl.ds(0, LANES)],
                                 basis[k, d + 2, rows, pl.ds(C - LANES, LANES)])
                if d:
                    both = pltpu.roll(both, STEPS * d, 1)
                west = jnp.where(group == d, both, west)
                east = jnp.where(group == (d - 1) % groups, both, east)
            pack_out[k, 0, rows] = west
            pack_out[k, 1, rows] = east
            return 0
        lax.fori_loop(0, R // ROWS_AT_ONCE, part, 0)

        @pl.when(has_w)
        def _():
            pack_copy(k, 0).start()

        @pl.when(has_e)
        def _():
            pack_copy(k, 1).start()

    def step(k, first=False, last=False):
        if last:
            pack_step(k)
        for c in range(chunks):
            wait_halo(k, c)
            if not last:
                edge_step(k, c, first)
                send_halo(k + 1, c)
        inner_step(k, first, last)
        if not last:
            pack_step(k)

    step(0, first=True)

    def middle(k, _):
        step(k)
        return 0

    lax.fori_loop(1, ITERS - 1, middle, 0)
    step(ITERS - 1, last=True)

    def exchange(ref, value, axis, me, count, send, recv):
        ref[me] = value
        def copy(o, slot):
            return pltpu.make_async_remote_copy(
                src_ref=ref.at[me], dst_ref=ref.at[me] if slot is None else ref.at[slot],
                send_sem=send.at[o], recv_sem=recv.at[me] if slot is None else recv.at[slot],
                device_id={axis: lax.rem(me + o, count)}, device_id_type=MESH)
        for o in range(1, count):
            copy(o, None).start()
        for o in range(1, count):
            copy(o, lax.rem(me + o, count)).wait_recv()
        total = ref[0]
        for j in range(1, count):
            total = total + ref[j]
        for o in range(1, count):
            copy(o, None).wait_send()
        return total

    n_mom = 2 * ITERS
    mine = jnp.sum(acc_ref[...].reshape(n_mom, SUB, LANES), axis=1)
    mine = jnp.concatenate([mine, jnp.zeros((sum_a.shape[1] - n_mom, LANES), jnp.float32)], axis=0)
    total = exchange(sum_a, mine, "tiles", me_t, nt, a_send, a_recv)
    total = exchange(sum_b, total, "dates", me_d, nd, b_send, b_recv)
    nu_ref[...] = jnp.broadcast_to(jnp.sum(total, axis=1, keepdims=True), nu_ref.shape)

    raw = [jnp.broadcast_to(nu_ref[j:j + 1, :], (SUB, LANES)) for j in range(n_mom)]
    unit = 1.0 / raw[0]
    raw = [value * unit for value in raw]
    nu = raw[:2]
    for k in range(1, ITERS):
        nu += [2.0 * raw[2 * k] - nu[0], 2.0 * raw[2 * k + 1] - nu[1]]
    h = [MID * nu[m] + (HALF * 0.5) * (nu[m + 1] + nu[abs(m - 1)]) for m in range(n_mom - 1)]
    M = {(i, j): 0.5 * (h[i + j] + h[j - i]) for i in range(ITERS) for j in range(i, ITERS)}
    b = list(nu[:ITERS])
    size = [M[i, i] for i in range(ITERS)]
    inverse, worst = [], None
    for i in range(ITERS):
        inverse.append(1.0 / M[i, i])
        ratio = jnp.where(M[i, i] > PIVOT_MIN * size[i], 1.0, 0.0)
        worst = ratio if worst is None else worst * ratio
        for j in range(i + 1, ITERS):
            f = M[i, j] * inverse[i]
            for q in range(j, ITERS):
                M[j, q] = M[j, q] - f * M[i, q]
            b[j] = b[j] - f * b[i]
    coef = [None] * ITERS
    for i in reversed(range(ITERS)):
        s = b[i]
        for q in range(i + 1, ITERS):
            s = s - M[i, q] * coef[q]
        coef[i] = s * inverse[i]
        c_ref[i] = coef[i]
    flag_ref[...] = worst

    for side, has in ((0, has_e), (1, has_w)):
        @pl.when(has)
        def _():
            for which in range(2):
                coef_copy(which, side).wait_recv()

            def one(k, _):
                pack_copy(k, side).wait_recv()
                return 0
            lax.fori_loop(0, ITERS, one, 0)

    wide = lax.broadcasted_iota(jnp.int32, (R, LANES), 1)
    is_e, is_w = wide < STEPS, wide >= LANES - STEPS

    def widened(ref, which):
        ends = jnp.where(is_e, coef_in[0, which], jnp.where(is_w, coef_in[1, which], 0.0))
        return jnp.concatenate([ref[...], ends], axis=1)

    dr, dc = widened(dr_ref, 0), widened(dc_ref, 1)
    row = lax.broadcasted_iota(jnp.int32, dr.shape, 0)
    coefs[0] = jnp.where(row > 0, dr, 0.0)
    coefs[1] = jnp.where(row < R - 1, dr, 0.0)
    coefs[2] = dc
    coefs[3] = 1.0 - 2.0 * dr - 2.0 * dc

    cs = [c_ref[i, 0:1, :] for i in range(ITERS)]
    for side in range(2):
        halo_ref[side] = functools.reduce(lambda a, b: a + b, [cs[i] * pack_in[i, side] for i in range(ITERS)])

    width = C + LANES

    def diffuse(d, _):
        parts = []
        for i in range(0, C, LANES):
            parts.append(functools.reduce(
                lambda a, b: a + b, [c_ref[k, 0:1, :] * basis[k, d + 2, :, pl.ds(i, LANES)] for k in range(ITERS)]))
        ends = jnp.where(wide // STEPS == d, halo_ref[0], halo_ref[1])
        ends = pltpu.roll(ends, lax.rem(LANES - STEPS * d, LANES), 1)
        parts.append(jnp.where(jnp.logical_or(is_e, is_w), ends, 0.0))
        f = jnp.concatenate(parts, axis=1)
        for _ in range(STEPS):
            f = (coefs[3] * f + coefs[0] * pltpu.roll(f, 1, 0) + coefs[1] * pltpu.roll(f, R - 1, 0)
                 + coefs[2] * (pltpu.roll(f, 1, 1) + pltpu.roll(f, width - 1, 1)))
        out_ref[d] = f[:, :C]
        return 0

    lax.fori_loop(0, D, diffuse, 0)

    def sent(k, _):
        for side, has, has_t in ((0, has_r, has_w), (1, has_l, has_e)):
            @pl.when(has)
            def _():
                for c in range(chunks):
                    halo_copy(k, c, side).wait_send()

            @pl.when(has_t)
            def _():
                pack_copy(k, side).wait_send()
        return 0

    lax.fori_loop(0, ITERS, sent, 0)
    for side, has in ((0, has_w), (1, has_e)):
        @pl.when(has)
        def _():
            for which in range(2):
                coef_copy(which, side).wait_send()


def fast(nd, nt, observed, cloud_mask, diffuse_rows, diffuse_cols):
    D, R, C = observed.shape
    chunks = 4
    slots = 24
    f32 = jnp.float32
    DMA = pltpu.SemaphoreType.DMA
    V = pl.BlockSpec(memory_space=pltpu.VMEM)
    return pl.pallas_call(
        functools.partial(kernel, nd, nt, chunks),
        out_shape=(jax.ShapeDtypeStruct((D, R, C), f32), jax.ShapeDtypeStruct((SUB, LANES), f32)),
        in_specs=[V] * 4,
        out_specs=(V, V),
        scratch_shapes=[
            pltpu.VMEM((ITERS, D + 4, R, C), f32),
            pltpu.VMEM((D, R, C), f32),
            pltpu.VMEM((ITERS, 2, R, LANES), f32),
            pltpu.VMEM((ITERS, 2, R, LANES), f32),
            pltpu.VMEM((2, 2, R, LANES), f32),
            pltpu.VMEM((4, R, C + LANES), f32),
            pltpu.VMEM((ITERS, 2, SUB, LANES), f32),
            pltpu.VMEM((nt, slots, LANES), f32),
            pltpu.VMEM((nd, slots, LANES), f32),
            pltpu.VMEM((slots, LANES), f32),
            pltpu.VMEM((ITERS, SUB, LANES), f32),
            pltpu.VMEM((2, R, LANES), f32),
            DMA((ITERS, chunks, 2)), DMA((ITERS, chunks, 2)),
            DMA((ITERS, 2)), DMA((ITERS, 2)),
            DMA((2, 2)), DMA((2, 2)),
            DMA((nt,)), DMA((nt,)),
            DMA((nd,)), DMA((nd,)),
        ],
        compiler_params=pltpu.CompilerParams(
            collective_id=0, has_side_effects=True, vmem_limit_bytes=60 * 1024 * 1024),
        name="smooth_and_fill",
    )(observed, cloud_mask, diffuse_rows, diffuse_cols)


def padded_by(cells, axis, dim, width):
    count = lax.axis_size(axis)
    head = lax.slice_in_dim(cells, 0, width, axis=dim)
    tail = lax.slice_in_dim(cells, cells.shape[dim] - width, cells.shape[dim], axis=dim)
    return jnp.concatenate(
        [
            lax.ppermute(tail, axis, [(i, i + 1) for i in range(count - 1)]),
            cells,
            lax.ppermute(head, axis, [(i + 1, i) for i in range(count - 1)]),
        ],
        axis=dim,
    )


def total_of(value):
    for axis in ("tiles", "dates"):
        count = lax.axis_size(axis)
        shift = 1
        while shift < count:
            value = value + lax.ppermute(value, axis, [(i, i ^ shift) for i in range(count)])
            shift *= 2
    return value


def plain(observed, cloud_mask, diffuse_rows, diffuse_cols):
    weights = cloud_mask.astype(jnp.float32) / 3.0 + 0.05
    rhs = weights * observed
    D = rhs.shape[0]
    dates = D * lax.axis_size("dates")
    place = lax.axis_index("dates") * D - 2 + jnp.arange(D + 2)
    inside = jnp.logical_and(place >= 0, place < dates - 2)[:, None, None]

    def time_operator(values):
        wide = padded_by(values, "dates", 0, 2)
        second = jnp.where(inside, wide[:-2] - 2.0 * wide[1:-1] + wide[2:], 0.0)
        return weights * values + smooth_weight * (second[:-2] - 2.0 * second[1:-1] + second[2:])

    def advance(step, state):
        smoothed, residual, direction, norm_now = state
        image = time_operator(direction)
        alpha = norm_now / total_of(jnp.sum(direction * image))
        smoothed = smoothed + alpha * direction
        residual = residual - alpha * image
        fresh = total_of(jnp.sum(residual * residual))
        direction = residual + fresh / norm_now * direction
        return (smoothed, residual, direction, fresh)

    state = (jnp.zeros_like(rhs), rhs, rhs, total_of(jnp.sum(rhs * rhs)))
    filled = lax.fori_loop(0, ITERS, advance, state)[0]

    def spread(step, filled):
        padded = jnp.pad(padded_by(filled, "tiles", 2, 1), ((0, 0), (1, 1), (0, 0)))
        centre = padded[:, 1:-1, 1:-1]
        along_rows = padded[:, 2:, 1:-1] + padded[:, :-2, 1:-1] - 2.0 * centre
        along_cols = padded[:, 1:-1, 2:] + padded[:, 1:-1, :-2] - 2.0 * centre
        return filled + diffuse_rows * along_rows + diffuse_cols * along_cols

    return lax.fori_loop(0, STEPS, spread, filled)


def solution(mesh):
    nd, nt = mesh.shape["dates"], mesh.shape["tiles"]

    def body(observed, cloud_mask, diffuse_rows, diffuse_cols):
        filled, good = fast(nd, nt, observed, cloud_mask, diffuse_rows, diffuse_cols)
        return lax.cond(
            good[0, 0] > 0.5,
            lambda: filled,
            lambda: plain(observed, cloud_mask, diffuse_rows, diffuse_cols),
        )

    in_specs = (
        P("dates", None, "tiles"),
        P("dates", None, "tiles"),
        P(None, "tiles"),
        P(None, "tiles"),
    )
    return jax.shard_map(body, mesh=mesh, in_specs=in_specs, out_specs=P("dates", None, "tiles"), check_vma=False)
```

time: 1090 us -> 73.1 us (0.07)
  blocking collectives: 909 us -> 0 us
  other arithmetic: 70.3 us -> 0 us
  Pallas kernels: 0 us -> 68.7 us
  starting transfers between devices: 39.3 us -> 0 us
  waiting for transfers between devices: 29.7 us -> 0 us
  loops' own time: 19.9 us -> 0.01 us
    psum x21 -> x0, blocking collectives: 847 us -> none  [the longest x11 433 us: squares(): return lax.psum(jnp.sum(residual * residual), ('dates', 'tiles'))]
    pallas_call x0 -> x1, Pallas kernels: none -> 68.7 us  [fast(): pl.pallas_call(functools.partial(kernel, nd, nt, chunks), out_shape=(jax....]
    all_to_all x2 -> x0, blocking collectives: 62.5 us -> none  [the longest x1 32.8 us: body(): lax.all_to_all(rhs, 'dates', split_axis=1, concat_axis=0, tiled=True)]
    add x25 -> x0, other arithmetic: 40.4 us -> none  [the longest x10 28.2 us: advance(): direction = residual + fresh / norm_now * direction]
    ppermute x8 -> x0, starting transfers between devices: 35.7 us -> none  [the longest x4 30.6 us: padded_2(): lax.ppermute(tail, axis, [(i, (i + 1) % count) for i in range(ends)])]
    reduce_sum x21 -> x0, other arithmetic: 26.7 us -> none  [the longest x10 13.5 us: advance(): curve = lax.psum(jnp.sum(direction * image), ('dates', 'tiles'))]
    all_to_all x1 -> x0, waiting for transfers between devices: 24 us -> none  [body(): lax.all_to_all(weights, 'dates', split_axis=1, concat_axis=0, tiled=True)]
    another operation x1, loops' own time: 19.9 us -> 0.01 us  [body(): lax.cond(good[0, 0] > 0.5, lambda: filled, lambda: plain(observed, cloud_...]
  transfers between devices with their start and end apart: 9 -> 0, of which waited for: 5 -> 0; matrix products, arithmetic and copies ran while one was open for 0% -> 0% of each run, Pallas kernels for 0% -> 0%
where the time goes in v1:
time: 73.1 us; the launch traced here: 72.9 us
  Pallas kernels  68.7 us (94%)
  local copies, waits for them, and re-layouts  3.51 us (5%)
    pallas_call x1, Pallas kernels, fast(): pl.pallas_call(functools.partial(kernel, nd, nt, chunks), out_shape=(jax....  68.7 us
    unnamed x9, local copies, waits for them, and re-layouts  2.32 us

profile of v1, /device:TPU:0, one launch (start us, length us, event | category | flops | bytes accessed | tf_op | source)
XLA Modules:
  0.0 72.9 jit_solution(15421680666725253734)
XLA Ops:
  0.0 0.0 copy-start.4
  0.0 0.0 copy-start.3
  0.0 0.0 copy-start.2
  0.0 0.0 copy-start.1
  0.0 68.7 %smooth_and_fill.1 = (f32[32,32,256]{2,1,0:T(8,128)}, f32[8,128]{1,0:T(8,128)}) custom-call(f32[32,32,256]{2,1,0:T(8,128)} %obs_ref.1, s32[32,32,256]{2,1,0:T(8,128)} %mask_ref.1, f32[32,256]{1,0:T(8,128)} %dr_ref.1, f32[32,256]{1,0:T(8,128)} %dc_ref.1), custom_call_target="tpu_custom_call" | custom-call | tf_op jit(solution)/shard_map/smooth_and_fill/pallas_call | solution.py:369
  68.7 1.2 %slice.67 = f32[1,1]{1,0:T(1,128)} slice(f32[8,128]{1,0:T(8,128)} %get-tuple-element.113), slice={[0:1], [0:1]} | slice | bytes 8 | tf_op jit(solution)/shard_map/slice | solution.py:465
  70.6 0.0 copy-done.4
  70.6 0.0 copy-done.3
  70.6 0.0 copy-done.2
  70.6 0.0 copy-done.1
  70.6 2.3 %copy.35 = f32[32,32,256]{2,1,0:T(8,128)} copy(f32[32,32,256]{2,1,0:T(8,128)} %get-tuple-element.115) | data formatting | bytes 2097152
  (1 shorter events, 0.0 us)
Async XLA Ops:
  0.0 70.6 %copy-start.4 = (f32[32,256]{1,0:T(8,128)S(1)}, f32[32,256]{1,0:T(8,128)}, u32[]{:S(2)}) copy-start(f32[32,256]{1,0:T(8,128)} %dc_ref.1) | copy-start | bytes 98308
  0.0 70.6 %copy-start.3 = (f32[32,256]{1,0:T(8,128)S(1)}, f32[32,256]{1,0:T(8,128)}, u32[]{:S(2)}) copy-start(f32[32,256]{1,0:T(8,128)} %dr_ref.1) | copy-start | bytes 98308
  0.0 70.6 %copy-start.2 = (s32[32,32,256]{2,1,0:T(8,128)S(1)}, s32[32,32,256]{2,1,0:T(8,128)}, u32[]{:S(2)}) copy-start(s32[32,32,256]{2,1,0:T(8,128)} %mask_ref.1) | copy-start | bytes 3145732
  0.0 70.6 %copy-start.1 = (f32[32,32,256]{2,1,0:T(8,128)S(1)}, f32[32,32,256]{2,1,0:T(8,128)}, u32[]{:S(2)}) copy-start(f32[32,32,256]{2,1,0:T(8,128)} %obs_ref.1) | copy-start | bytes 3145732

commit v2 on v1

--- a/solution.py
+++ b/solution.py
@@ -11,7 +11,6 @@
 STEPS = 4
 LANES = 128
 SUB = 8
-ROWS_AT_ONCE = 32
 
 smooth_weight = 4.0
 LOW, HIGH = 0.05, 65.05
@@ -20,11 +19,12 @@
 MESH = pl.DeviceIdType.MESH
 
 
-def kernel(nd, nt, chunks, obs_ref, mask_ref, dr_ref, dc_ref, out_ref, flag_ref,
+def kernel(nd, nt, row_chunks, col_chunks, obs_ref, mask_ref, dr_ref, dc_ref, out_ref, flag_ref,
            basis, weights, pack_out, pack_in, coef_in, coefs, acc_ref, sum_a, sum_b, nu_ref, c_ref, halo_ref,
            halo_send, halo_recv, pack_send, pack_recv, coef_send, coef_recv, a_send, a_recv, b_send, b_recv):
     D, R, C = obs_ref.shape
-    RC = R // chunks
+    chunks = row_chunks * col_chunks
+    RC, CC = R // row_chunks, C // col_chunks
     me_d, me_t = lax.axis_index("dates"), lax.axis_index("tiles")
     has_l, has_r = me_d > 0, me_d < nd - 1
     has_w, has_e = me_t > 0, me_t < nt - 1
@@ -34,7 +34,8 @@
     barrier = pltpu.get_barrier_semaphore()
     for o in range(1, nt):
         pl.semaphore_signal(barrier, inc=1, device_id={"tiles": lax.rem(me_t + o, nt)}, device_id_type=MESH)
-    for o in range(1, nd):
+    greeted = (1, nd - 1) if 2 < nd < ITERS else range(1, nd)
+    for o in greeted:
         pl.semaphore_signal(barrier, inc=1, device_id={"dates": lax.rem(me_d + o, nd)}, device_id_type=MESH)
 
     def start_plane(t, _):
@@ -43,40 +44,18 @@
         basis[0, t + 2] = w * obs_ref[t]
         return 0
 
-    lax.fori_loop(0, D, start_plane, 0)
-
-    def clear(ref, ks, at):
-        def one(k, _):
-            ref[(k,) + at] = jnp.zeros_like(ref[(k,) + at])
-            return 0
-        lax.fori_loop(0, ks, one, 0)
-
-    @pl.when(jnp.logical_not(has_l))
-    def _():
-        clear(basis, ITERS, (pl.ds(0, 2),))
-
-    @pl.when(jnp.logical_not(has_r))
-    def _():
-        clear(basis, ITERS, (pl.ds(D + 2, 2),))
-
-    @pl.when(jnp.logical_not(has_e))
-    def _():
-        clear(pack_in, ITERS, (0,))
-        coef_in[0] = jnp.zeros_like(coef_in[0])
-
-    @pl.when(jnp.logical_not(has_w))
-    def _():
-        clear(pack_in, ITERS, (1,))
-        coef_in[1] = jnp.zeros_like(coef_in[1])
-
-    pl.semaphore_wait(barrier, nt - 1 + nd - 1)
+    edges = sorted({0, 1, D - 2, D - 1})
+    for t in edges:
+        start_plane(t, 0)
+
+    pl.semaphore_wait(barrier, nt - 1 + len(greeted))
 
     def halo_copy(k, c, side):
-        rows = pl.ds(c * RC, RC)
+        rows, cols = pl.ds(c // col_chunks * RC, RC), pl.ds(c % col_chunks * CC, CC)
         if side == 0:
-            src, dst, to = basis.at[k, pl.ds(D, 2), rows], basis.at[k, pl.ds(0, 2), rows], me_d + 1
+            src, dst, to = basis.at[k, pl.ds(D, 2), rows, cols], basis.at[k, pl.ds(0, 2), rows, cols], me_d + 1
         else:
-            src, dst, to = basis.at[k, pl.ds(2, 2), rows], basis.at[k, pl.ds(D + 2, 2), rows], me_d - 1
+            src, dst, to = basis.at[k, pl.ds(2, 2), rows, cols], basis.at[k, pl.ds(D + 2, 2), rows, cols], me_d - 1
         return pltpu.make_async_remote_copy(
             src_ref=src, dst_ref=dst, send_sem=halo_send.at[k, c, side], recv_sem=halo_recv.at[k, c, side],
             device_id={"dates": to}, device_id_type=MESH)
@@ -93,23 +72,25 @@
             src_ref=ref.at[:, cols], dst_ref=coef_in.at[side, which], send_sem=coef_send.at[side, which],
             recv_sem=coef_recv.at[side, which], device_id={"tiles": me_t - 1 if side == 0 else me_t + 1}, device_id_type=MESH)
 
-    def send_halo(k, c):
+    def send_halo(k, c, both=True):
         @pl.when(has_r)
         def _():
             halo_copy(k, c, 0).start()
 
-        @pl.when(has_l)
-        def _():
-            halo_copy(k, c, 1).start()
-
-    def wait_halo(k, c):
+        if both:
+            @pl.when(has_l)
+            def _():
+                halo_copy(k, c, 1).start()
+
+    def wait_halo(k, c, both=True):
         @pl.when(has_l)
         def _():
             halo_copy(k, c, 0).wait_recv()
 
-        @pl.when(has_r)
-        def _():
-            halo_copy(k, c, 1).wait_recv()
+        if both:
+            @pl.when(has_r)
+            def _():
+                halo_copy(k, c, 1).wait_recv()
 
     for c in range(chunks):
         send_halo(0, c)
@@ -123,6 +104,32 @@
     def _():
         for which in range(2):
             coef_copy(which, 1).start()
+
+    lax.fori_loop(2, D - 2, start_plane, 0)
+
+    def clear(ref, ks, at):
+        def one(k, _):
+            ref[(k,) + at] = jnp.zeros_like(ref[(k,) + at])
+            return 0
+        lax.fori_loop(0, ks, one, 0)
+
+    @pl.when(jnp.logical_not(has_l))
+    def _():
+        clear(basis, ITERS, (pl.ds(0, 2),))
+
+    @pl.when(jnp.logical_not(has_r))
+    def _():
+        clear(basis, ITERS, (pl.ds(D + 2, 2),))
+
+    @pl.when(jnp.logical_not(has_e))
+    def _():
+        clear(pack_in, ITERS, (0,))
+        coef_in[0] = jnp.zeros_like(coef_in[0])
+
+    @pl.when(jnp.logical_not(has_w))
+    def _():
+        clear(pack_in, ITERS, (1,))
+        coef_in[1] = jnp.zeros_like(coef_in[1])
 
     def second(v, j):
         u = v[j] - 2.0 * v[j + 1] + v[j + 2]
@@ -132,70 +139,87 @@
             u = u * mask_r
         return u
 
-    def next_plane(k, t, rows, v, u, first):
+    def next_plane(k, t, rows, cols, v, u, first):
         back = u[t - 2] - 2.0 * u[t - 1] + u[t]
-        image = weights[t, rows] * v[t] + smooth_weight * back
+        image = weights[t, rows, cols] * v[t] + smooth_weight * back
         scale = 1.0 if first else 2.0
         new = (scale / HALF) * image - (scale * MID / HALF) * v[t]
         if not first:
-            new = new - basis[k - 1, t + 2, rows]
+            new = new - basis[k - 1, t + 2, rows, cols]
         return new
 
-    edges = sorted({0, 1, D - 2, D - 1})
+    def place(c, r):
+        return (pl.ds(pl.multiple_of(c // col_chunks * RC + r * SUB, SUB), SUB), pl.ds(c % col_chunks * CC, CC))
 
     def edge_step(k, c, first):
         def part(r, _):
-            rows = pl.ds(pl.multiple_of(c * RC + r * SUB, SUB), SUB)
+            rows, cols = place(c, r)
             v, u = {}, {}
             for t in edges:
                 for j in range(t - 2, t + 3):
                     if j not in v:
-                        v[j] = basis[k, j + 2, rows]
+                        v[j] = basis[k, j + 2, rows, cols]
                 for j in range(t - 2, t + 1):
                     if j not in u:
                         u[j] = second(v, j)
-                basis[k + 1, t + 2, rows] = next_plane(k, t, rows, v, u, first)
+                basis[k + 1, t + 2, rows, cols] = next_plane(k, t, rows, cols, v, u, first)
             return 0
         if RC == SUB:
             part(0, 0)
         else:
             lax.fori_loop(0, RC // SUB, part, 0)
 
-    def inner_step(k, first, last):
+    def inner_step(k, c, first, last):
         def part(r, carry):
             own, cross = carry
-            rows = pl.ds(pl.multiple_of(r * SUB, SUB), SUB)
+            rows, cols = place(c, r)
             v, u = {}, {}
             for t in range(D):
-                stored = t in edges and not last
+                stored = t in edges
                 for j in range(t - 2, t + 3):
                     if j not in v and not (stored and j != t):
-                        v[j] = basis[k, j + 2, rows]
+                        v[j] = basis[k, j + 2, rows, cols]
                 if stored:
-                    new = basis[k + 1, t + 2, rows]
+                    new = basis[k + 1, t + 2, rows, cols]
                 else:
                     for j in range(t - 2, t + 1):
                         if j not in u:
                             u[j] = second(v, j)
-                    new = next_plane(k, t, rows, v, u, first)
-                    if not last:
-                        basis[k + 1, t + 2, rows] = new
+                    new = next_plane(k, t, rows, cols, v, u, first)
+                    basis[k + 1, t + 2, rows, cols] = new
                 own = own + v[t] * v[t]
                 cross = cross + v[t] * new
             return own, cross
-        zero = jnp.zeros((SUB, C), jnp.float32)
-        own, cross = lax.fori_loop(0, R // SUB, part, (zero, zero))
+
+        def last_part(r, carry):
+            own, energy = carry
+            rows, cols = place(c, r)
+            v = {j: basis[k, j + 2, rows, cols] for j in range(-2, D)}
+            bend = jnp.zeros_like(own)
+            for t in range(D):
+                u = second(v, t - 2)
+                bend = bend + u * u
+                square = v[t] * v[t]
+                own = own + square
+                energy = energy + weights[t, rows, cols] * square
+            return own, energy + smooth_weight * bend
+
+        if last:
+            part = last_part
+        zero = jnp.zeros((SUB, CC), jnp.float32)
+        own, cross = part(0, (zero, zero)) if RC == SUB else lax.fori_loop(0, RC // SUB, part, (zero, zero))
         for which, acc in ((0, own), (1, cross)):
-            acc_ref[k, which] = functools.reduce(lambda a, b: a + b, [acc[:, i:i + LANES] for i in range(0, C, LANES)])
-
-    lane = lax.broadcasted_iota(jnp.int32, (ROWS_AT_ONCE, LANES), 1)
+            acc = functools.reduce(lambda a, b: a + b, [acc[:, i:i + LANES] for i in range(0, CC, LANES)])
+            acc_ref[k, which] = acc if c == 0 else acc_ref[k, which] + acc
+
+    lane = lax.broadcasted_iota(jnp.int32, (SUB, LANES), 1)
     group = lane // STEPS
     groups = LANES // STEPS
 
-    def pack_step(k):
+    def pack_step(k, c):
         def part(r, _):
-            rows = pl.ds(pl.multiple_of(r * ROWS_AT_ONCE, ROWS_AT_ONCE), ROWS_AT_ONCE)
-            west = east = jnp.zeros((ROWS_AT_ONCE, LANES), jnp.float32)
+            rows = pl.ds(pl.multiple_of(c * RC + r * SUB, SUB), SUB)
+            west = east = jnp.zeros((SUB, LANES), jnp.float32)
             for d in range(D):
                 both = jnp.where(lane < LANES // 2, basis[k, d + 2, rows, pl.ds(0, LANES)],
                                  basis[k, d + 2, rows, pl.ds(C - LANES, LANES)])
@@ -206,8 +230,12 @@
             pack_out[k, 0, rows] = west
             pack_out[k, 1, rows] = east
             return 0
-        lax.fori_loop(0, R // ROWS_AT_ONCE, part, 0)
-
+        if RC == SUB:
+            part(0, 0)
+        else:
+            lax.fori_loop(0, RC // SUB, part, 0)
+
+    def send_pack(k):
         @pl.when(has_w)
         def _():
             pack_copy(k, 0).start()
@@ -216,17 +244,21 @@
         def _():
             pack_copy(k, 1).start()
 
-    def step(k, first=False, last=False):
+    def step(k, first=False, last=False, before_last=False):
         if last:
-            pack_step(k)
+            for c in range(row_chunks):
+                pack_step(k, c)
+            send_pack(k)
         for c in range(chunks):
-            wait_halo(k, c)
+            wait_halo(k, c, not last)
             if not last:
                 edge_step(k, c, first)
-                send_halo(k + 1, c)
-        inner_step(k, first, last)
+                send_halo(k + 1, c, not before_last)
+            inner_step(k, c, first, last)
+            if not last and c % col_chunks == col_chunks - 1:
+                pack_step(k, c // col_chunks)
         if not last:
-            pack_step(k)
+            send_pack(k)
 
     step(0, first=True)
 
@@ -234,10 +266,11 @@
         step(k)
         return 0
 
-    lax.fori_loop(1, ITERS - 1, middle, 0)
+    lax.fori_loop(1, ITERS - 2, middle, 0)
+    step(ITERS - 2, before_last=True)
     step(ITERS - 1, last=True)
 
-    def exchange(ref, value, axis, me, count, send, recv):
+    def exchange(ref, value, axis, me, count, send, recv, meanwhile):
         ref[me] = value
         def copy(o, slot):
             return pltpu.make_async_remote_copy(
@@ -246,6 +279,7 @@
                 device_id={axis: lax.rem(me + o, count)}, device_id_type=MESH)
         for o in range(1, count):
             copy(o, None).start()
+        meanwhile()
         for o in range(1, count):
             copy(o, lax.rem(me + o, count)).wait_recv()
         total = ref[0]
@@ -255,16 +289,63 @@
             copy(o, None).wait_send()
         return total
 
+    wide = lax.broadcasted_iota(jnp.int32, (R, LANES), 1)
+    is_e, is_w = wide < STEPS, wide >= LANES - STEPS
+
+    def ready():
+        for side, has in ((0, has_e), (1, has_w)):
+            @pl.when(has)
+            def _():
+                for which in range(2):
+                    coef_copy(which, side).wait_recv()
+
+                def one(k, _):
+                    pack_copy(k, side).wait_recv()
+                    return 0
+                lax.fori_loop(0, ITERS, one, 0)
+
+        def widened(ref, which):
+            ends = jnp.where(is_e, coef_in[0, which], jnp.where(is_w, coef_in[1, which], 0.0))
+            return jnp.concatenate([ref[...], ends], axis=1)
+
+        dr, dc = widened(dr_ref, 0), widened(dc_ref, 1)
+        row = lax.broadcasted_iota(jnp.int32, dr.shape, 0)
+        coefs[0] = jnp.where(row > 0, dr, 0.0)
+        coefs[1] = jnp.where(row < R - 1, dr, 0.0)
+        coefs[2] = dc
+        coefs[3] = 1.0 - 2.0 * dr - 2.0 * dc
+
+    def drained():
+        def sent(k, _):
+            for side, has, has_t in ((0, has_r, has_w), (1, has_l, has_e)):
+                @pl.when(has if side == 0 else jnp.logical_and(has, k < ITERS - 1))
+                def _():
+                    for c in range(chunks):
+                        halo_copy(k, c, side).wait_send()
+
+                @pl.when(has_t)
+                def _():
+                    pack_copy(k, side).wait_send()
+            return 0
+
+        lax.fori_loop(0, ITERS, sent, 0)
+        for side, has in ((0, has_w), (1, has_e)):
+            @pl.when(has)
+            def _():
+                for which in range(2):
+                    coef_copy(which, side).wait_send()
+
     n_mom = 2 * ITERS
     mine = jnp.sum(acc_ref[...].reshape(n_mom, SUB, LANES), axis=1)
     mine = jnp.concatenate([mine, jnp.zeros((sum_a.shape[1] - n_mom, LANES), jnp.float32)], axis=0)
-    total = exchange(sum_a, mine, "tiles", me_t, nt, a_send, a_recv)
-    total = exchange(sum_b, total, "dates", me_d, nd, b_send, b_recv)
+    total = exchange(sum_a, mine, "tiles", me_t, nt, a_send, a_recv, ready)
+    total = exchange(sum_b, total, "dates", me_d, nd, b_send, b_recv, drained)
     nu_ref[...] = jnp.broadcast_to(jnp.sum(total, axis=1, keepdims=True), nu_ref.shape)
 
     raw = [jnp.broadcast_to(nu_ref[j:j + 1, :], (SUB, LANES)) for j in range(n_mom)]
     unit = 1.0 / raw[0]
     raw = [value * unit for value in raw]
+    raw[-1] = (2.0 / HALF) * (raw[-1] - MID * raw[-2]) - raw[-3]
     nu = raw[:2]
     for k in range(1, ITERS):
         nu += [2.0 * raw[2 * k] - nu[0], 2.0 * raw[2 * k + 1] - nu[1]]
@@ -289,32 +370,7 @@
             s = s - M[i, q] * coef[q]
         coef[i] = s * inverse[i]
         c_ref[i] = coef[i]
-    flag_ref[...] = worst
-
-    for side, has in ((0, has_e), (1, has_w)):
-        @pl.when(has)
-        def _():
-            for which in range(2):
-                coef_copy(which, side).wait_recv()
-
-            def one(k, _):
-                pack_copy(k, side).wait_recv()
-                return 0
-            lax.fori_loop(0, ITERS, one, 0)
-
-    wide = lax.broadcasted_iota(jnp.int32, (R, LANES), 1)
-    is_e, is_w = wide < STEPS, wide >= LANES - STEPS
-
-    def widened(ref, which):
-        ends = jnp.where(is_e, coef_in[0, which], jnp.where(is_w, coef_in[1, which], 0.0))
-        return jnp.concatenate([ref[...], ends], axis=1)
-
-    dr, dc = widened(dr_ref, 0), widened(dc_ref, 1)
-    row = lax.broadcasted_iota(jnp.int32, dr.shape, 0)
-    coefs[0] = jnp.where(row > 0, dr, 0.0)
-    coefs[1] = jnp.where(row < R - 1, dr, 0.0)
-    coefs[2] = dc
-    coefs[3] = 1.0 - 2.0 * dr - 2.0 * dc
+    flag_ref[0] = jnp.min(worst)
 
     cs = [c_ref[i, 0:1, :] for i in range(ITERS)]
     for side in range(2):
@@ -337,40 +393,22 @@
         out_ref[d] = f[:, :C]
         return 0
 
-    lax.fori_loop(0, D, diffuse, 0)
-
-    def sent(k, _):
-        for side, has, has_t in ((0, has_r, has_w), (1, has_l, has_e)):
-            @pl.when(has)
-            def _():
-                for c in range(chunks):
-                    halo_copy(k, c, side).wait_send()
-
-            @pl.when(has_t)
-            def _():
-                pack_copy(k, side).wait_send()
-        return 0
-
-    lax.fori_loop(0, ITERS, sent, 0)
-    for side, has in ((0, has_w), (1, has_e)):
-        @pl.when(has)
-        def _():
-            for which in range(2):
-                coef_copy(which, side).wait_send()
+    lax.fori_loop(0, D, diffuse, 0, unroll=4 if D * R <= 1024 else 1)
 
 
 def fast(nd, nt, observed, cloud_mask, diffuse_rows, diffuse_cols):
     D, R, C = observed.shape
-    chunks = 4
+    row_chunks, col_chunks = 4, 1
+    chunks = row_chunks * col_chunks
     slots = 24
     f32 = jnp.float32
     DMA = pltpu.SemaphoreType.DMA
     V = pl.BlockSpec(memory_space=pltpu.VMEM)
     return pl.pallas_call(
-        functools.partial(kernel, nd, nt, chunks),
-        out_shape=(jax.ShapeDtypeStruct((D, R, C), f32), jax.ShapeDtypeStruct((SUB, LANES), f32)),
+        functools.partial(kernel, nd, nt, row_chunks, col_chunks),
+        out_shape=(jax.ShapeDtypeStruct((D, R, C), f32), jax.ShapeDtypeStruct((1,), f32)),
         in_specs=[V] * 4,
-        out_specs=(V, V),
+        out_specs=(V, pl.BlockSpec(memory_space=pltpu.SMEM)),
         scratch_shapes=[
             pltpu.VMEM((ITERS, D + 4, R, C), f32),
             pltpu.VMEM((D, R, C), f32),
@@ -462,7 +500,7 @@
     def body(observed, cloud_mask, diffuse_rows, diffuse_cols):
         filled, good = fast(nd, nt, observed, cloud_mask, diffuse_rows, diffuse_cols)
         return lax.cond(
-            good[0, 0] > 0.5,
+            good[0] > 0.5,
             lambda: filled,
             lambda: plain(observed, cloud_mask, diffuse_rows, diffuse_cols),
         )

time: 73.1 us -> 62.6 us (0.86)
  Pallas kernels: 68.7 us -> 59.5 us
  local copies, waits for them, and re-layouts: 3.51 us -> 2.32 us
    pallas_call x1, Pallas kernels: 68.7 us -> 59.5 us  [fast(): pl.pallas_call(functools.partial(kernel, nd, nt, row_chunks, col_chunks),...]
    slice x1 -> x0, local copies, waits for them, and re-layouts: 1.19 us -> none  [body(): good[0, 0] > 0.5]
where the time goes in v2:
time: 62.6 us; the launch traced here: 62.5 us
  Pallas kernels  59.5 us (95%)
  local copies, waits for them, and re-layouts  2.32 us (4%)
  between operations  0.67 us (1%)
    pallas_call x1, Pallas kernels, fast(): pl.pallas_call(functools.partial(kernel, nd, nt, row_chunks, col_chunks),...  59.5 us
    unnamed x9, local copies, waits for them, and re-layouts  2.32 us

profile of v2, /device:TPU:0, one launch (start us, length us, event | category | flops | bytes accessed | tf_op | source)
XLA Modules:
  0.0 62.5 jit_solution(2990547332706990735)
XLA Ops:
  0.0 0.0 copy-start.4
  0.0 0.0 copy-start.3
  0.0 0.0 copy-start.2
  0.0 0.0 copy-start.1
  0.0 59.5 %smooth_and_fill.1 = (f32[32,32,256]{2,1,0:T(8,128)}, f32[1]{0:T(128)}) custom-call(f32[32,32,256]{2,1,0:T(8,128)} %obs_ref.1, s32[32,32,256]{2,1,0:T(8,128)} %mask_ref.1, f32[32,256]{1,0:T(8,128)} %dr_ref.1, f32[32,256]{1,0:T(8,128)} %dc_ref.1), custom_call_target="tpu_custom_call" | custom-call | tf_op jit(solution)/shard_map/smooth_and_fill/pallas_call | solution.py:407
  60.1 0.0 copy-done.4
  60.1 0.0 copy-done.3
  60.1 0.0 copy-done.2
  60.1 0.0 copy-done.1
  60.2 2.3 %copy.35 = f32[32,32,256]{2,1,0:T(8,128)} copy(f32[32,32,256]{2,1,0:T(8,128)} %get-tuple-element.115) | data formatting | bytes 2097152
  (1 shorter events, 0.0 us)
Async XLA Ops:
  0.0 60.1 %copy-start.4 = (f32[32,256]{1,0:T(8,128)S(1)}, f32[32,256]{1,0:T(8,128)}, u32[]{:S(2)}) copy-start(f32[32,256]{1,0:T(8,128)} %dc_ref.1) | copy-start | bytes 98308
  0.0 60.1 %copy-start.3 = (f32[32,256]{1,0:T(8,128)S(1)}, f32[32,256]{1,0:T(8,128)}, u32[]{:S(2)}) copy-start(f32[32,256]{1,0:T(8,128)} %dr_ref.1) | copy-start | bytes 98308
  0.0 60.1 %copy-start.2 = (s32[32,32,256]{2,1,0:T(8,128)S(1)}, s32[32,32,256]{2,1,0:T(8,128)}, u32[]{:S(2)}) copy-start(s32[32,32,256]{2,1,0:T(8,128)} %mask_ref.1) | copy-start | bytes 3145732
  0.0 60.1 %copy-start.1 = (f32[32,32,256]{2,1,0:T(8,128)S(1)}, f32[32,32,256]{2,1,0:T(8,128)}, u32[]{:S(2)}) copy-start(f32[32,32,256]{2,1,0:T(8,128)} %obs_ref.1) | copy-start | bytes 3145732

commit v3 on v2

--- a/solution.py
+++ b/solution.py
@@ -21,7 +21,7 @@
 
 def kernel(nd, nt, row_chunks, col_chunks, obs_ref, mask_ref, dr_ref, dc_ref, out_ref, flag_ref,
            basis, weights, pack_out, pack_in, coef_in, coefs, acc_ref, sum_a, sum_b, nu_ref, c_ref, halo_ref,
-           halo_send, halo_recv, pack_send, pack_recv, coef_send, coef_recv, a_send, a_recv, b_send, b_recv):
+           halo_send, halo_recv, pack_send, pack_recv, coef_send, coef_recv, a_send, a_recv, b_send, b_recv, result, out_sem):
     D, R, C = obs_ref.shape
     chunks = row_chunks * col_chunks
     RC, CC = R // row_chunks, C // col_chunks
@@ -390,10 +390,18 @@
         for _ in range(STEPS):
             f = (coefs[3] * f + coefs[0] * pltpu.roll(f, 1, 0) + coefs[1] * pltpu.roll(f, R - 1, 0)
                  + coefs[2] * (pltpu.roll(f, 1, 1) + pltpu.roll(f, width - 1, 1)))
-        out_ref[d] = f[:, :C]
+        result[d] = f[:, :C]
         return 0
 
-    lax.fori_loop(0, D, diffuse, 0, unroll=4 if D * R <= 1024 else 1)
+    some = D // 4 if D % 16 == 0 else D
+    leaving = []
+    for at in range(0, D, some):
+        lax.fori_loop(at, at + some, diffuse, 0, unroll=4 if D * R <= 1024 else 1)
+        leaving.append(pltpu.make_async_copy(
+            result.at[pl.ds(at, some)], out_ref.at[pl.ds(at, some)], out_sem.at[at // some]))
+        leaving[-1].start()
+    for copy in leaving:
+        copy.wait()
 
 
 def fast(nd, nt, observed, cloud_mask, diffuse_rows, diffuse_cols):
@@ -408,7 +416,7 @@
         functools.partial(kernel, nd, nt, row_chunks, col_chunks),
         out_shape=(jax.ShapeDtypeStruct((D, R, C), f32), jax.ShapeDtypeStruct((1,), f32)),
         in_specs=[V] * 4,
-        out_specs=(V, pl.BlockSpec(memory_space=pltpu.SMEM)),
+        out_specs=(pl.BlockSpec(memory_space=pl.ANY), pl.BlockSpec(memory_space=pltpu.SMEM)),
         scratch_shapes=[
             pltpu.VMEM((ITERS, D + 4, R, C), f32),
             pltpu.VMEM((D, R, C), f32),
@@ -427,6 +435,7 @@
             DMA((2, 2)), DMA((2, 2)),
             DMA((nt,)), DMA((nt,)),
             DMA((nd,)), DMA((nd,)),
+            pltpu.VMEM((D, R, C), f32), DMA((4,)),
         ],
         compiler_params=pltpu.CompilerParams(
             collective_id=0, has_side_effects=True, vmem_limit_bytes=60 * 1024 * 1024),

time: 62.6 us -> 63 us (level)
  no operation moved by 1% of the time
where the time goes in v3:
time: 63 us; the launch traced here: 62.9 us
  Pallas kernels  59.7 us (95%)
  local copies, waits for them, and re-layouts  2.32 us (4%)
  between operations  0.67 us (1%)
    pallas_call x1, Pallas kernels, fast(): pl.pallas_call(functools.partial(kernel, nd, nt, row_chunks, col_chunks),...  59.7 us
    unnamed x9, local copies, waits for them, and re-layouts  2.32 us

profile of v3, /device:TPU:0, one launch (start us, length us, event | category | flops | bytes accessed | tf_op | source)
XLA Modules:
  0.0 62.9 jit_solution(6624572178689255036)
XLA Ops:
  0.0 0.0 copy-start.4
  0.0 0.0 copy-start.3
  0.0 0.0 copy-start.2
  0.0 0.0 copy-start.1
  0.0 59.7 %smooth_and_fill.1 = (f32[32,32,256]{2,1,0:T(8,128)}, f32[1]{0:T(128)}) custom-call(f32[32,32,256]{2,1,0:T(8,128)} %obs_ref.1, s32[32,32,256]{2,1,0:T(8,128)} %mask_ref.1, f32[32,256]{1,0:T(8,128)} %dr_ref.1, f32[32,256]{1,0:T(8,128)} %dc_ref.1), custom_call_target="tpu_custom_call" | custom-call | tf_op jit(solution)/shard_map/smooth_and_fill/pallas_call | solution.py:415
  60.3 0.0 copy-done.4
  60.4 0.0 copy-done.3
  60.4 0.0 copy-done.2
  60.4 0.0 copy-done.1
  60.4 0.2 conditional.1
  60.6 2.3 %copy.35 = f32[32,32,256]{2,1,0:T(8,128)} copy(f32[32,32,256]{2,1,0:T(8,128)} %get-tuple-element.115) | data formatting | bytes 2097152
Async XLA Ops:
  0.0 60.3 %copy-start.4 = (f32[32,256]{1,0:T(8,128)S(1)}, f32[32,256]{1,0:T(8,128)}, u32[]{:S(2)}) copy-start(f32[32,256]{1,0:T(8,128)} %dc_ref.1) | copy-start | bytes 98308
  0.0 60.4 %copy-start.3 = (f32[32,256]{1,0:T(8,128)S(1)}, f32[32,256]{1,0:T(8,128)}, u32[]{:S(2)}) copy-start(f32[32,256]{1,0:T(8,128)} %dr_ref.1) | copy-start | bytes 98308
  0.0 60.4 %copy-start.2 = (s32[32,32,256]{2,1,0:T(8,128)S(1)}, s32[32,32,256]{2,1,0:T(8,128)}, u32[]{:S(2)}) copy-start(s32[32,32,256]{2,1,0:T(8,128)} %mask_ref.1) | copy-start | bytes 3145732
  0.0 60.4 %copy-start.1 = (f32[32,32,256]{2,1,0:T(8,128)S(1)}, f32[32,32,256]{2,1,0:T(8,128)}, u32[]{:S(2)}) copy-start(f32[32,32,256]{2,1,0:T(8,128)} %obs_ref.1) | copy-start | bytes 3145732
